TPU v7x, 1024 devices: a whole 4x4x32 slice. The times are simulated.
1024 devices in a mesh: ep: 16 (over x_hi, y, core), dp: 64 (over x_lo, z).
Axes of the slice: x: 4 (x_hi: 2, x_lo: 2; x = x_hi * 2 + x_lo), y: 4, z: 32, core: 2. Of those that a mesh axis runs over, the one named last changes fastest.
Arguments:
- fwd_tokens: bfloat16 [16384, 2048], P(('ep', 'dp')), may hold values from -6 to 6
- fwd_routes: int32 [16384, 8], P(('ep', 'dp')), may hold values from 0 to 15, as said below
- fwd_weights: float32 [16384, 8], P(('ep', 'dp')), may hold values from 0.05 to 0.4
- bwd_grads: bfloat16 [16384, 2048], P(('ep', 'dp')), may hold values from -24 to 24
- bwd_routes: int32 [16384, 8], P(('ep', 'dp')), may hold values from 0 to 15, as said below
- bwd_weights: float32 [16384, 8], P(('ep', 'dp')), may hold values from 0.05 to 0.4
- bwd_saved: bfloat16 [16, 8192, 2048], P('ep', 'dp'), may hold values from -6 to 6
- w_gate: bfloat16 [16, 2048, 384], P('ep'), may hold values from -0.125 to 0.125
- w_up: bfloat16 [16, 2048, 384], P('ep'), may hold values from -0.125 to 0.125
- w_down: bfloat16 [16, 384, 2048], P('ep'), may hold values from -0.3125 to 0.3125
Outputs:
- fwd_out: bfloat16 [16384, 2048], P(('ep', 'dp'))
- bwd_input_grad: bfloat16 [16384, 2048], P(('ep', 'dp'))
- down_grad: float32 [16, 2048, 384], P('ep', 'dp')
Inputs may be any that keep to these rules, and one draw needn't show every extreme that they name: `fwd_routes`: each token names 8 different experts, and the 16 tokens of each aligned block (one device's tokens) name every expert exactly 8 times. `bwd_routes`: each token names 8 different experts, and the 16 tokens of each aligned block (one device's tokens) name every expert exactly 8 times.
All inputs are finite; a program needn't handle non-finite values.
Results may differ from a plain program's by a relative error of at most 0.0064.
Values may be sent and summed in bfloat16 or wider, within the bound.
No kernel may reach another device: no remote copies, remote signals or barrier semaphores. Data moves between devices by JAX's collectives and lax.ppermute only.
A program may use at most 32 MiB of HBM per device.

v0:
```python
import jax
import jax.numpy as jnp
from jax import lax
from jax.sharding import PartitionSpec as P


def slot_tables(routes, weights, experts):
    token_count, picks = routes.shape
    slot_count = token_count * picks // experts
    hits = routes[:, :, None] == jnp.arange(experts, dtype=jnp.int32)[None, None, :]
    member = jnp.sum(hits.astype(jnp.int32), axis=1)
    before = jnp.cumsum(member, axis=0) - member
    slot_ids = jnp.arange(slot_count, dtype=jnp.int32)[None, :, None]
    chosen = (member.T[:, None, :] == 1) & (before.T[:, None, :] == slot_ids)
    mixing = jnp.sum(jnp.where(hits, weights[:, :, None], 0.0), axis=1)
    return (chosen, mixing)


def expert_forward(arrived, w_gate, w_up, w_down):
    sources, local_experts, slot_count, model_width = arrived.shape
    rows_in = arrived[:, 0].reshape(sources * slot_count, model_width)
    gate_pre = jnp.dot(rows_in, w_gate[0], preferred_element_type=jnp.float32)
    up_pre = jnp.dot(rows_in, w_up[0], preferred_element_type=jnp.float32)
    hidden = (jax.nn.silu(gate_pre) * up_pre).astype(jnp.bfloat16)
    expert_out = jnp.dot(hidden, w_down[0], preferred_element_type=jnp.float32).astype(jnp.bfloat16)
    results = [expert_out.reshape(sources, slot_count, model_width)]
    return jnp.stack(results, axis=1)


def expert_backward(cotangent, bwd_saved, w_gate, w_up, w_down):
    sources, local_experts, slot_count, model_width = cotangent.shape
    contract_last = (((1,), (1,)), ((), ()))
    cot_rows = cotangent[:, 0].reshape(sources * slot_count, model_width)
    saved_rows = bwd_saved[0]
    gate_pre = jnp.dot(saved_rows, w_gate[0], preferred_element_type=jnp.float32)
    up_pre = jnp.dot(saved_rows, w_up[0], preferred_element_type=jnp.float32)
    sigma = jax.nn.sigmoid(gate_pre)
    hidden = (gate_pre * sigma * up_pre).astype(jnp.bfloat16)
    dact = lax.dot_general(cot_rows, w_down[0], contract_last, preferred_element_type=jnp.float32)
    dgate = (dact * up_pre * sigma * (1.0 + gate_pre * (1.0 - sigma))).astype(jnp.bfloat16)
    dup_rows = (dact * gate_pre * sigma).astype(jnp.bfloat16)
    row_grad = lax.dot_general(dgate, w_gate[0], contract_last, preferred_element_type=jnp.float32)
    row_grad = row_grad + lax.dot_general(
        dup_rows, w_up[0], contract_last, preferred_element_type=jnp.float32
    )
    row_grads = [row_grad.astype(jnp.bfloat16).reshape(sources, slot_count, model_width)]
    cot_list = [cot_rows]
    hidden_list = [hidden]
    return (
        jnp.stack(row_grads, axis=1),
        jnp.stack(cot_list, axis=0),
        jnp.stack(hidden_list, axis=0),
    )


def weight_terms(cot_all, hidden_all):
    return jnp.einsum("ern,erf->enf", cot_all, hidden_all, preferred_element_type=jnp.float32)


def on_device(
    fwd_tokens,
    fwd_routes,
    fwd_weights,
    bwd_grads,
    bwd_routes,
    bwd_weights,
    bwd_saved,
    w_gate,
    w_up,
    w_down,
):
    groups = lax.axis_size("ep")
    local_experts = w_gate.shape[0]
    experts = groups * local_experts
    model_width = fwd_tokens.shape[1]
    fwd_chosen, fwd_mixing = slot_tables(fwd_routes, fwd_weights, experts)
    bwd_chosen, bwd_mixing = slot_tables(bwd_routes, bwd_weights, experts)
    slot_count = fwd_chosen.shape[1]
    layout = (groups, local_experts, slot_count, model_width)
    fwd_select = fwd_chosen.astype(jnp.bfloat16)
    bwd_select = bwd_chosen.astype(jnp.bfloat16)
    send_tokens = jnp.einsum(
        "est,td->esd", fwd_select, fwd_tokens, preferred_element_type=jnp.float32
    )
    send_tokens = send_tokens.astype(jnp.bfloat16).reshape(layout)
    bwd_scale = jnp.sum(jnp.where(bwd_chosen, bwd_mixing.T[:, None, :], 0.0), axis=2)
    picked_grads = jnp.einsum(
        "est,td->esd", bwd_select, bwd_grads, preferred_element_type=jnp.float32
    )
    send_grads = (picked_grads * bwd_scale[:, :, None]).astype(jnp.bfloat16).reshape(layout)
    arrived = lax.all_to_all(send_tokens, "ep", split_axis=0, concat_axis=0, tiled=True)
    expert_out = expert_forward(arrived, w_gate, w_up, w_down)
    returned = lax.all_to_all(expert_out, "ep", split_axis=0, concat_axis=0, tiled=True)
    returned = returned.reshape(experts, slot_count, model_width)
    per_expert = jnp.einsum(
        "est,esd->etd", fwd_select, returned, preferred_element_type=jnp.float32
    )
    combined = jnp.sum(fwd_mixing.T[:, :, None] * per_expert, axis=0)
    fwd_out = combined.astype(jnp.bfloat16)
    arrived = lax.all_to_all(send_grads, "ep", split_axis=0, concat_axis=0, tiled=True)
    row_grads, cot_all, hidden_all = expert_backward(arrived, bwd_saved, w_gate, w_up, w_down)
    home_rows = lax.all_to_all(row_grads, "ep", split_axis=0, concat_axis=0, tiled=True)
    down_grad = lax.psum_scatter(
        weight_terms(cot_all, hidden_all), "dp", scatter_dimension=1, tiled=True
    )
    home_rows = home_rows.reshape(experts, slot_count, model_width)
    input_grad = jnp.einsum(
        "est,esd->td", bwd_select, home_rows, preferred_element_type=jnp.float32
    )
    bwd_input_grad, down_grad = (input_grad.astype(jnp.bfloat16), down_grad)
    return (fwd_out, bwd_input_grad, down_grad)


def solution(mesh):
    in_specs = (
        P(("ep", "dp"), None),
        P(("ep", "dp"), None),
        P(("ep", "dp"), None),
        P(("ep", "dp"), None),
        P(("ep", "dp"), None),
        P(("ep", "dp"), None),
        P("ep", "dp", None),
        P("ep", None, None),
        P("ep", None, None),
        P("ep", None, None),
    )
    out_specs = (P(("ep", "dp"), None), P(("ep", "dp"), None), P("ep", "dp", None))
    return jax.shard_map(
        on_device, mesh=mesh, in_specs=in_specs, out_specs=out_specs, check_vma=False
    )
```

profile of v0, /device:TPU:8, one launch (start us, length us, event | category | flops | bytes accessed | tf_op | source)
XLA Modules:
  0.0 318.1 jit_solution(10313410083535036746)
XLA Ops:
  7.2 0.9 convert_reduce_fusion
  8.1 0.1 copy.22
  8.3 0.7 select_reduce_fusion.1
  9.1 0.1 copy.27
  9.2 0.1 copy.25
  9.3 1.9 fusion.5
  11.2 17.0 %all-to-all-start.2 = ((bf16[16,1,8,2048]{3,2,1,0:T(8,128)(2,1)}), bf16[16,1,8,2048]{3,2,1,0:T(8,128)(2,1)}, u32[]{:S(2)}, u32[]{:S(2)}) async-start(bf16[16,1,8,2048]{3,2,1,0:T(8,128)(2,1)} %fusion.5), calls=%async_computation.2 | async-start | bytes 1048576 | tf_op jit(solution)/shard_map/all_to_all | solution.py:100
  28.3 1.5 fusion.17
  29.9 0.5 fusion.11
  30.4 6.7 %all-to-all-done.2 = bf16[16,1,8,2048]{3,2,1,0:T(8,128)(2,1)} async-done(((bf16[16,1,8,2048]{3,2,1,0:T(8,128)(2,1)}), bf16[16,1,8,2048]{3,2,1,0:T(8,128)(2,1)}, u32[]{:S(2)}, u32[]{:S(2)}) %all-to-all-start.2) | async-done | bytes 524320 | tf_op jit(solution)/shard_map/all_to_all | solution.py:100
  37.1 3.3 %convolution_bitcast_fusion = f32[1,2048,384]{2,1,0:T(8,128)} fusion(bf16[16,1,8,2048]{3,2,1,0:T(8,128)(2,1)} %all-to-all-done.2, f32[128,384]{1,0:T(8,128)S(1)} %fusion.11, f32[128,384]{1,0:T(8,128)S(1)} %fusion.17), kind=kOutput, calls=%fused_computation | convolution fusion | flops 201621504 | bytes 4063232 | tf_op jit(solution)/shard_map/ern,erf->enf/dot_general | solution.py:57
  40.4 0.7 copy-done.8
  41.1 0.1 copy.17
  41.2 0.6 reduce_window_sum.17
  41.8 1.3 subtract_bitcast_fusion.1
  43.1 0.8 copy.19
  43.9 0.6 copy-done.10
  44.5 1.1 fusion.2
  45.6 15.0 %all_to_all.20 = bf16[16,1,8,2048]{3,2,1,0:T(8,128)(2,1)S(1)} all-to-all(bf16[16,1,8,2048]{3,2,1,0:T(8,128)(2,1)S(1)} %fusion.2), channel_id=1, replica_groups=mesh['ep'=16,'dp'=64] {'ep'}, dimensions={0} | all-to-all | bytes 1048576 | tf_op jit(solution)/shard_map/all_to_all | solution.py:91
  60.5 0.8 copy-done.2
  61.3 1.1 fusion.19
  62.5 3.3 %fusion.3 = bf16[16,1,8,2048]{3,2,1,0:T(8,128)(2,1)} fusion(bf16[1,384,2048]{2,1,0:T(8,128)(2,1)} %param.19, bf16[1,2048,384]{2,1,0:T(8,128)(2,1)S(1)} %copy-done, bf16[16,1,8,2048]{3,2,1,0:T(8,128)(2,1)} %copy-done.2, f32[128,384]{1,0:T(8,128)} %fusion.19), kind=kOutput, calls=%fused_computation.9 | convolution fusion | flops 403210240 | bytes 4390912 | tf_op jit(solution)/shard_map/dot_general | solution.py:25
  65.8 7.8 %all-to-all-start.1 = ((bf16[16,1,8,2048]{3,2,1,0:T(8,128)(2,1)}), bf16[16,1,8,2048]{3,2,1,0:T(8,128)(2,1)}, u32[]{:S(2)}, u32[]{:S(2)}) async-start(bf16[16,1,8,2048]{3,2,1,0:T(8,128)(2,1)} %fusion.3), calls=%async_computation.1 | async-start | bytes 1048576 | tf_op jit(solution)/shard_map/all_to_all | solution.py:93
  73.6 2.2 fusion.7
  75.8 0.6 fusion.15
  76.4 1.4 fusion.4
  77.9 5.4 %all-to-all-done.1 = bf16[16,1,8,2048]{3,2,1,0:T(8,128)(2,1)} async-done(((bf16[16,1,8,2048]{3,2,1,0:T(8,128)(2,1)}), bf16[16,1,8,2048]{3,2,1,0:T(8,128)(2,1)}, u32[]{:S(2)}, u32[]{:S(2)}) %all-to-all-start.1) | async-done | bytes 524320 | tf_op jit(solution)/shard_map/all_to_all | solution.py:93
  83.2 7.4 %all-to-all-start.3 = ((bf16[16,1,8,2048]{3,2,1,0:T(8,128)(2,1)}), bf16[16,1,8,2048]{3,2,1,0:T(8,128)(2,1)S(1)}, u32[]{:S(2)}, u32[]{:S(2)}) async-start(bf16[16,1,8,2048]{3,2,1,0:T(8,128)(2,1)} %fusion.4), calls=%async_computation.3 | async-start | bytes 1048576 | tf_op jit(solution)/shard_map/all_to_all | solution.py:102
  90.7 2.2 fusion.21
  92.9 7.1 %all-to-all-done.3 = bf16[16,1,8,2048]{3,2,1,0:T(8,128)(2,1)S(1)} async-done(((bf16[16,1,8,2048]{3,2,1,0:T(8,128)(2,1)}), bf16[16,1,8,2048]{3,2,1,0:T(8,128)(2,1)S(1)}, u32[]{:S(2)}, u32[]{:S(2)}) %all-to-all-start.3) | async-done | bytes 524320 | tf_op jit(solution)/shard_map/all_to_all | solution.py:102
  100.0 1.0 fusion.6
  101.0 210.2 %reduce-scatter.2.cloned.1.call-done = f32[1,32,384]{2,1,0:T(8,128)} async-done(((f32[1,2048,384]{2,1,0:T(8,128)}), f32[1,32,384]{2,1,0:T(8,128)}) %reduce-scatter.2.cloned.1.call-update) | async-done | bytes 49168 | tf_op jit(solution)/shard_map/reduce_scatter | solution.py:103
  (35 shorter events, 0.4 us)
Async XLA Ops:
  7.2 22.7 %copy-start = (bf16[1,2048,384]{2,1,0:T(8,128)(2,1)S(1)}, bf16[1,2048,384]{2,1,0:T(8,128)(2,1)}, u32[]{:S(2)}) copy-start(bf16[1,2048,384]{2,1,0:T(8,128)(2,1)} %param.18) | copy-start | bytes 4718596
  7.2 21.1 %copy-start.1 = (bf16[1,2048,384]{2,1,0:T(8,128)(2,1)S(1)}, bf16[1,2048,384]{2,1,0:T(8,128)(2,1)}, u32[]{:S(2)}) copy-start(bf16[1,2048,384]{2,1,0:T(8,128)(2,1)} %param.17) | copy-start | bytes 4718596
  8.2 0.9 copy-start.6
  8.3 20.0 %copy-start.4 = (s32[16,16]{0,1:T(8,128)}, s32[16,16]{0,1:T(8,128)S(1)}, u32[]{:S(2)}) copy-start(s32[16,16]{0,1:T(8,128)S(1)} %subtract_bitcast_fusion) | copy-start | bytes 3076
  11.2 25.9 %all-to-all-start.2 = ((bf16[16,1,8,2048]{3,2,1,0:T(8,128)(2,1)}), bf16[16,1,8,2048]{3,2,1,0:T(8,128)(2,1)}, u32[]{:S(2)}, u32[]{:S(2)}) async-start(bf16[16,1,8,2048]{3,2,1,0:T(8,128)(2,1)} %fusion.5), calls=%async_computation.2 | async-start | bytes 1048576 | tf_op jit(solution)/shard_map/all_to_all | solution.py:100
  28.3 283.0 %reduce-scatter.2.cloned.1.call-start = ((), (), s32[]{:S(2)}) async-start(), calls=%async_computation.5 | async-start | bytes 3194880 | tf_op jit(solution)/shard_map/reduce_scatter | solution.py:103
  28.3 1.6 copy-start.3
  40.4 0.7 copy-start.8
  43.9 0.6 copy-start.10
  60.5 0.8 copy-start.2
  65.8 17.4 %all-to-all-start.1 = ((bf16[16,1,8,2048]{3,2,1,0:T(8,128)(2,1)}), bf16[16,1,8,2048]{3,2,1,0:T(8,128)(2,1)}, u32[]{:S(2)}, u32[]{:S(2)}) async-start(bf16[16,1,8,2048]{3,2,1,0:T(8,128)(2,1)} %fusion.3), calls=%async_computation.1 | async-start | bytes 1048576 | tf_op jit(solution)/shard_map/all_to_all | solution.py:93
  76.4 14.3 %copy-start.9 = (s32[16,8]{0,1:T(8,128)S(1)}, s32[16,8]{0,1:T(8,128)}, u32[]{:S(2)}) copy-start(s32[16,8]{0,1:T(8,128)} %param.11) | copy-start | bytes 1540
  76.4 14.3 %copy-start.12 = (f32[16,8]{0,1:T(8,128)S(1)}, f32[16,8]{0,1:T(8,128)}, u32[]{:S(2)}) copy-start(f32[16,8]{0,1:T(8,128)} %param.12) | copy-start | bytes 1540
  76.4 14.3 %copy-start.11 = (pred[16,16]{1,0:T(8,128)(4,1)S(1)}, pred[16,16]{1,0:T(8,128)(4,1)}, u32[]{:S(2)}) copy-start(pred[16,16]{1,0:T(8,128)(4,1)} %copy-done.10) | copy-start | bytes 772
  77.9 22.1 %copy-start.5 = (s32[16,16]{0,1:T(8,128)S(1)}, s32[16,16]{0,1:T(8,128)}, u32[]{:S(2)}) copy-start(s32[16,16]{0,1:T(8,128)} %copy-done.4) | copy-start | bytes 3076
  77.9 22.1 %copy-start.7 = (pred[16,16]{0,1:T(8,128)(4,1)S(1)}, pred[16,16]{0,1:T(8,128)(4,1)}, u32[]{:S(2)}) copy-start(pred[16,16]{0,1:T(8,128)(4,1)} %copy-done.6) | copy-start | bytes 772
  83.2 16.7 %all-to-all-start.3 = ((bf16[16,1,8,2048]{3,2,1,0:T(8,128)(2,1)}), bf16[16,1,8,2048]{3,2,1,0:T(8,128)(2,1)S(1)}, u32[]{:S(2)}, u32[]{:S(2)}) async-start(bf16[16,1,8,2048]{3,2,1,0:T(8,128)(2,1)} %fusion.4), calls=%async_computation.3 | async-start | bytes 1048576 | tf_op jit(solution)/shard_map/all_to_all | solution.py:102
Sparse Core Ops, SparseCore 0:
  40.6 270.6 reduce-scatter.1
where the time goes:
time: 319 us; the launch traced here: 318 us
  waiting for transfers between devices  229 us (72%)
  starting transfers between devices  32.3 us (10%)
  matrix products  20.3 us (6%)
  blocking collectives  15 us (5%)
  between operations  14.2 us (4%)
  other arithmetic  3.63 us (1%)
  local copies, waits for them, and re-layouts  3.32 us (1%)
    reduce_scatter x1, waiting for transfers between devices, on_device(): lax.psum_scatter(weight_terms(cot_all, hidden_all), 'dp', scatter_dimensi...  210 us
    all_to_all x1, starting transfers between devices, on_device(): lax.all_to_all(send_grads, 'ep', split_axis=0, concat_axis=0, tiled=True)  17 us
    all_to_all x1, blocking collectives, on_device(): lax.all_to_all(send_tokens, 'ep', split_axis=0, concat_axis=0, tiled=True)  15 us
    all_to_all x1, starting transfers between devices, on_device(): lax.all_to_all(expert_out, 'ep', split_axis=0, concat_axis=0, tiled=True)  7.77 us
    all_to_all x1, starting transfers between devices, on_device(): lax.all_to_all(row_grads, 'ep', split_axis=0, concat_axis=0, tiled=True)  7.45 us
    all_to_all x1, waiting for transfers between devices, on_device(): lax.all_to_all(row_grads, 'ep', split_axis=0, concat_axis=0, tiled=True)  7.06 us
    all_to_all x1, waiting for transfers between devices, on_device(): lax.all_to_all(send_grads, 'ep', split_axis=0, concat_axis=0, tiled=True)  6.74 us
  transfers between devices with their start and end apart: 4, of which 4 were waited for; matrix products, arithmetic and copies ran while one was open for 6% of the time, Pallas kernels for 0%

commit v1 on v0

v1 whole, which is shorter than its diff:
```python
import jax
import jax.numpy as jnp
from jax import lax
from jax.experimental import pallas as pl
from jax.experimental.pallas import tpu as pltpu
from jax.sharding import PartitionSpec as P

EXPERTS = 16
SLOTS = 8
NEAR = 4
BF16, F32 = jnp.bfloat16, jnp.float32


def slot_matrix(routes_t, weights_t):
    picks, tokens = routes_t.shape
    rows = EXPERTS * SLOTS
    row = lax.broadcasted_iota(jnp.int32, (rows, tokens), 0)
    expert, slot = row // SLOTS, row % SLOTS
    member = jnp.zeros((rows, tokens), F32)
    mixing = jnp.zeros((rows, tokens), F32)
    for k in range(picks):
        hit = routes_t[k : k + 1, :] == expert
        member = member + jnp.where(hit, 1.0, 0.0)
        mixing = mixing + jnp.where(hit, weights_t[k : k + 1, :], 0.0)
    earlier = lax.broadcasted_iota(jnp.int32, (tokens, tokens), 0) < lax.broadcasted_iota(
        jnp.int32, (tokens, tokens), 1
    )
    before = jnp.dot(
        member.astype(BF16), jnp.where(earlier, 1.0, 0.0).astype(BF16), preferred_element_type=F32
    )
    chosen = (member > 0.5) & (before.astype(jnp.int32) == slot)
    return jnp.where(chosen, 1.0, 0.0), jnp.where(chosen, mixing, 0.0)


def select_kernel(scaled, routes_ref, weights_ref, x_ref, out_ref):
    chosen, mixing = slot_matrix(routes_ref[...], weights_ref[...])
    scale = jnp.sum(mixing, axis=1, keepdims=True)
    chosen = chosen.astype(BF16)
    for c in range(0, x_ref.shape[1], 256):
        rows = jnp.dot(chosen, x_ref[:, c : c + 256], preferred_element_type=F32)
        if scaled:
            rows = rows * scale
        out_ref[:, c : c + 256] = rows.astype(BF16)


def select(routes, weights, x, scaled):
    import functools

    rows, width = EXPERTS * SLOTS, x.shape[1]
    return pl.pallas_call(
        functools.partial(select_kernel, scaled),
        out_shape=jax.ShapeDtypeStruct((rows, width), BF16),
        cost_estimate=pl.CostEstimate(flops=2 * rows * 16 * width, bytes_accessed=rows * width * 4, transcendentals=0),
        name="select_scaled" if scaled else "select_plain",
    )(routes.T, weights.T, x)


def combine_kernel(weighted, routes_ref, weights_ref, rows_ref, out_ref):
    chosen, mixing = slot_matrix(routes_ref[...], weights_ref[...])
    contract_rows = (((0,), (0,)), ((), ()))
    if weighted:
        high = mixing.astype(BF16)
        rest = mixing - high.astype(F32)
        middle = rest.astype(BF16)
        low = (rest - middle.astype(F32)).astype(BF16)
        parts = [low, middle, high]
    else:
        parts = [chosen.astype(BF16)]
    parts = [p.astype(F32).T.astype(BF16) for p in parts]
    for c in range(0, rows_ref.shape[1], 512):
        rows = rows_ref[:, c : c + 512]
        total = jnp.dot(parts[0], rows, preferred_element_type=F32)
        for p in parts[1:]:
            total = total + jnp.dot(p, rows, preferred_element_type=F32)
        out_ref[:, c : c + 512] = total.astype(BF16)


def combine(routes, weights, rows, weighted):
    import functools

    return pl.pallas_call(
        functools.partial(combine_kernel, weighted),
        out_shape=jax.ShapeDtypeStruct((routes.shape[0], rows.shape[1]), BF16),
        cost_estimate=pl.CostEstimate(flops=10**7, bytes_accessed=rows.size * 2, transcendentals=0),
        name="combine_weighted" if weighted else "combine_plain",
    )(routes.T, weights.T, rows)


def split_kernel(cot_ref, out_ref):
    members, columns, rows = out_ref.shape
    halves = members // NEAR
    fars = cot_ref.shape[1] // (halves * 128)
    sub = 128 // NEAR
    for half in range(halves):
        for far in range(fars):
            at = (half * fars + far) * 128
            tile = cot_ref[:, at : at + 128].astype(F32).T.astype(BF16)
            for k in range(NEAR):
                out_ref[half * NEAR + k, far * sub : (far + 1) * sub, :] = tile[k * sub : (k + 1) * sub, :]


def split_columns(cot, members):
    rows, width = cot.shape
    return pl.pallas_call(
        split_kernel,
        out_shape=jax.ShapeDtypeStruct((members, width // members, rows), BF16),
        cost_estimate=pl.CostEstimate(flops=10**6, bytes_accessed=rows * width * 4, transcendentals=0),
        name="split_columns",
    )(cot)


def grad_kernel(cot_ref, act_ref, out_ref):
    total = jnp.zeros(out_ref.shape, F32)
    for s in range(cot_ref.shape[0]):
        total = total + jnp.dot(cot_ref[s], act_ref[s], preferred_element_type=F32)
    out_ref[...] = total.astype(BF16)


def grad_part(cot_t, act):
    members, columns, rows = cot_t.shape
    return pl.pallas_call(
        grad_kernel,
        out_shape=jax.ShapeDtypeStruct((columns, act.shape[2]), BF16),
        cost_estimate=pl.CostEstimate(
            flops=2 * members * columns * rows * act.shape[2], bytes_accessed=cot_t.size * 4, transcendentals=0
        ),
        name="grad_part",
    )(cot_t, act)


def on_device(
    fwd_tokens, fwd_routes, fwd_weights, bwd_grads, bwd_routes, bwd_weights, bwd_saved, w_gate, w_up, w_down
):
    dp = lax.axis_size("dp")
    depth = dp // 2
    fars = depth // NEAR
    near = [[x * depth + f * NEAR + k for x in range(2) for k in range(NEAR)] for f in range(fars)]
    far = [[x * depth + f * NEAR + k for f in range(fars)] for x in range(2) for k in range(NEAR)]
    width = fwd_tokens.shape[1]
    rows = EXPERTS * SLOTS
    contract_last = (((1,), (1,)), ((), ()))
    gate_w, up_w, down_w = w_gate[0], w_up[0], w_down[0]

    def swap(x, axis="ep", groups=None):
        return lax.all_to_all(x, axis, split_axis=0, concat_axis=0, tiled=True, axis_index_groups=groups)

    def exchange(x):
        return swap(x.reshape(EXPERTS, SLOTS, width)).reshape(rows, width)

    gate_b = jnp.dot(bwd_saved[0], gate_w, preferred_element_type=F32)
    up_b = jnp.dot(bwd_saved[0], up_w, preferred_element_type=F32)
    sig = jax.nn.sigmoid(gate_b)
    act_b = (gate_b * sig * up_b).astype(BF16)
    act_all = swap(jnp.broadcast_to(act_b[None], (len(near[0]),) + act_b.shape), "dp", near)

    cot = exchange(select(bwd_routes, bwd_weights, bwd_grads, True))
    cot_all = swap(split_columns(cot, len(near[0])), "dp", near)

    rows_a = exchange(select(fwd_routes, fwd_weights, fwd_tokens, False))

    dact = lax.dot_general(cot, down_w, contract_last, preferred_element_type=F32)
    dgate = (dact * up_b * sig * (1.0 + gate_b * (1.0 - sig))).astype(BF16)
    dup = (dact * gate_b * sig).astype(BF16)
    row_b = lax.dot_general(dgate, gate_w, contract_last, preferred_element_type=F32)
    row_b = row_b + lax.dot_general(dup, up_w, contract_last, preferred_element_type=F32)
    back_b = exchange(row_b.astype(BF16))

    part = grad_part(cot_all, act_all)
    part = swap(part.reshape(fars, part.shape[0] // fars, part.shape[1]), "dp", far)
    down_grad = jnp.sum(part.astype(F32), axis=0)[None]

    gate_a = jnp.dot(rows_a, gate_w, preferred_element_type=F32)
    up_a = jnp.dot(rows_a, up_w, preferred_element_type=F32)
    act_a = (jax.nn.silu(gate_a) * up_a).astype(BF16)
    row_a = jnp.dot(act_a, down_w, preferred_element_type=F32).astype(BF16)
    back_a = exchange(row_a)

    fwd_out = combine(fwd_routes, fwd_weights, back_a, True)
    input_grad = combine(bwd_routes, bwd_weights, back_b, False)
    return fwd_out, input_grad, down_grad


def solution(mesh):
    in_specs = (P(("ep", "dp"), None),) * 6 + (P("ep", "dp", None),) + (P("ep", None, None),) * 3
    out_specs = (P(("ep", "dp"), None), P(("ep", "dp"), None), P("ep", "dp", None))
    return jax.shard_map(on_device, mesh=mesh, in_specs=in_specs, out_specs=out_specs, check_vma=False)
```

time: 319 us -> 177 us (0.55)
  the two profiles are of different devices: /device:TPU:8 before, /device:TPU:34 now
where the time goes in v1:
time: 177 us; the launch traced here: 175 us
  waiting for transfers between devices  76.5 us (43%)
  starting transfers between devices  44.8 us (25%)
  blocking collectives  26.8 us (15%)
  Pallas kernels  13.3 us (8%)
  matrix products  11.6 us (7%)
    all_to_all x6, waiting for transfers between devices, swap(): lax.all_to_all(x, axis, split_axis=0, concat_axis=0, tiled=True, axis_ind...  76.5 us
    all_to_all x6, starting transfers between devices, swap(): lax.all_to_all(x, axis, split_axis=0, concat_axis=0, tiled=True, axis_ind...  44.8 us
    all_to_all x1, blocking collectives, swap(): lax.all_to_all(x, axis, split_axis=0, concat_axis=0, tiled=True, axis_ind...  26.8 us
    pallas_call x2, Pallas kernels, select(): pl.pallas_call(functools.partial(select_kernel, scaled), out_shape=jax.Sh...  4.39 us
    pallas_call x2, Pallas kernels, combine(): pl.pallas_call(functools.partial(combine_kernel, weighted), out_shape=jax...  4.34 us
  transfers between devices with their start and end apart: 6, of which 6 were waited for; matrix products, arithmetic and copies ran while one was open for 7% of the time, Pallas kernels for 6%

profile of v1, /device:TPU:34, one launch (start us, length us, event | category | flops | bytes accessed | tf_op | source)
XLA Modules:
  0.0 175.5 jit_solution(17820933963552045621)
XLA Ops:
  0.6 0.0 copy-start
  0.7 2.3 %select_scaled.1 = bf16[128,2048]{1,0:T(8,128)(2,1)} custom-call(s32[8,16]{1,0:T(8,128)} %bitcast.62, f32[8,16]{1,0:T(8,128)} %bitcast.64, bf16[16,2048]{1,0:T(8,128)(2,1)} %x_ref.3), custom_call_target="tpu_custom_call" | custom-call | flops 8388608 | bytes 1048576 | tf_op jit(solution)/shard_map/select_scaled/pallas_call | solution.py:50
  2.9 6.2 %all-to-all-start.2 = ((bf16[16,8,2048]{2,1,0:T(8,128)(2,1)}), bf16[16,8,2048]{2,1,0:T(8,128)(2,1)}, u32[]{:S(2)}, u32[]{:S(2)}) async-start(bf16[16,8,2048]{2,1,0:T(8,128)(2,1)} %bitcast.59), calls=%async_computation.2 | async-start | bytes 1048576 | tf_op jit(solution)/shard_map/all_to_all | solution.py:145
  9.1 2.1 %select_plain.1 = bf16[128,2048]{1,0:T(8,128)(2,1)} custom-call(s32[8,16]{1,0:T(8,128)} %bitcast.66, f32[8,16]{1,0:T(8,128)} %bitcast.68, bf16[16,2048]{1,0:T(8,128)(2,1)} %x_ref.2), custom_call_target="tpu_custom_call" | custom-call | flops 8388608 | bytes 1048576 | tf_op jit(solution)/shard_map/select_plain/pallas_call | solution.py:50
  11.2 1.5 fusion.13
  12.8 0.0 copy-done
  12.8 0.0 copy-done.3
  12.8 1.1 multiply_convert_fusion
  13.9 7.6 %all-to-all-done.2 = bf16[16,8,2048]{2,1,0:T(8,128)(2,1)} async-done(((bf16[16,8,2048]{2,1,0:T(8,128)(2,1)}), bf16[16,8,2048]{2,1,0:T(8,128)(2,1)}, u32[]{:S(2)}, u32[]{:S(2)}) %all-to-all-start.2) | async-done | bytes 524320 | tf_op jit(solution)/shard_map/all_to_all | solution.py:145
  21.5 4.2 %all-to-all-start = ((bf16[16,8,2048]{2,1,0:T(8,128)(2,1)}), bf16[16,8,2048]{2,1,0:T(8,128)(2,1)}, u32[]{:S(2)}, u32[]{:S(2)}) async-start(bf16[16,8,2048]{2,1,0:T(8,128)(2,1)} %bitcast.57), calls=%async_computation | async-start | bytes 1048576 | tf_op jit(solution)/shard_map/all_to_all | solution.py:145
  25.8 2.2 %fusion.3 = f32[128,384]{1,0:T(8,128)S(1)} fusion(bf16[1,384,2048]{2,1,0:T(8,128)(2,1)} %param.19, bf16[16,8,2048]{2,1,0:T(8,128)(2,1)} %all-to-all-done.2), kind=kOutput, calls=%fused_computation.5 | convolution fusion | flops 201326592 | bytes 2293760 | tf_op jit(solution)/shard_map/dot_general | solution.py:161
  28.0 0.6 fusion.11
  28.6 1.5 fusion.2
  30.1 8.0 %all-to-all-done = bf16[16,8,2048]{2,1,0:T(8,128)(2,1)} async-done(((bf16[16,8,2048]{2,1,0:T(8,128)(2,1)}), bf16[16,8,2048]{2,1,0:T(8,128)(2,1)}, u32[]{:S(2)}, u32[]{:S(2)}) %all-to-all-start) | async-done | bytes 524320 | tf_op jit(solution)/shard_map/all_to_all | solution.py:145
  38.1 4.2 %all-to-all-start.3 = ((bf16[16,8,2048]{2,1,0:T(8,128)(2,1)}), bf16[16,8,2048]{2,1,0:T(8,128)(2,1)}, u32[]{:S(2)}, u32[]{:S(2)}) async-start(bf16[16,8,2048]{2,1,0:T(8,128)(2,1)} %fusion.2), calls=%async_computation.3 | async-start | bytes 1048576 | tf_op jit(solution)/shard_map/all_to_all | solution.py:145
  42.4 2.0 %split_columns.1 = bf16[8,256,128]{2,1,0:T(8,128)(2,1)} custom-call(bf16[128,2048]{1,0:T(8,128)(2,1)} %bitcast.12.cot_ref), custom_call_target="tpu_custom_call" | custom-call | flops 1000000 | bytes 1048576 | tf_op jit(solution)/shard_map/split_columns/pallas_call | solution.py:104
  44.4 10.3 %all-to-all-done.3 = bf16[16,8,2048]{2,1,0:T(8,128)(2,1)} async-done(((bf16[16,8,2048]{2,1,0:T(8,128)(2,1)}), bf16[16,8,2048]{2,1,0:T(8,128)(2,1)}, u32[]{:S(2)}, u32[]{:S(2)}) %all-to-all-start.3) | async-done | bytes 524320 | tf_op jit(solution)/shard_map/all_to_all | solution.py:145
  54.7 26.8 %all_to_all.35.cot_ref = bf16[8,256,128]{2,1,0:T(8,128)(2,1)} all-to-all(bf16[8,256,128]{2,1,0:T(8,128)(2,1)} %split_columns.1), channel_id=1, replica_groups={{0,1,2,3,32,33,34,35},{4,5,6,7,36,37,38,39},{8,9,10,11,40,41,42,43},{12..., dimensions={0} | all-to-all | bytes 1048576 | tf_op jit(solution)/shard_map/all_to_all | solution.py:145
  81.5 1.0 broadcast_in_dim.4
  82.5 7.2 %all-to-all-start.5 = ((bf16[8,128,384]{2,1,0:T(8,128)(2,1)}), bf16[8,128,384]{2,1,0:T(8,128)(2,1)}, u32[]{:S(2)}, u32[]{:S(2)}) async-start(bf16[8,128,384]{2,1,0:T(8,128)(2,1)} %broadcast_in_dim.4), calls=%async_computation.5 | async-start | bytes 1572864 | tf_op jit(solution)/shard_map/all_to_all | solution.py:145
  89.7 1.5 fusion.15
  91.2 3.2 %fusion.1 = bf16[16,8,2048]{2,1,0:T(8,128)(2,1)} fusion(bf16[1,384,2048]{2,1,0:T(8,128)(2,1)} %param.19, bf16[1,2048,384]{2,1,0:T(8,128)(2,1)S(1)} %copy-done, bf16[16,8,2048]{2,1,0:T(8,128)(2,1)} %all-to-all-done, f32[128,384]{1,0:T(8,128)S(1)} %fusion.15), kind=kOutput, calls=%fused_computation.3 | convolution fusion | flops 403210240 | bytes 4390912 | tf_op jit(solution)/shard_map/dot_general | solution.py:175
  94.4 11.0 %all-to-all-done.5.act_ref = bf16[8,128,384]{2,1,0:T(8,128)(2,1)} async-done(((bf16[8,128,384]{2,1,0:T(8,128)(2,1)}), bf16[8,128,384]{2,1,0:T(8,128)(2,1)}, u32[]{:S(2)}, u32[]{:S(2)}) %all-to-all-start.5) | async-done | bytes 786464 | tf_op jit(solution)/shard_map/all_to_all | solution.py:145
  105.4 4.3 %all-to-all-start.1 = ((bf16[16,8,2048]{2,1,0:T(8,128)(2,1)}), bf16[16,8,2048]{2,1,0:T(8,128)(2,1)S(1)}, u32[]{:S(2)}, u32[]{:S(2)}) async-start(bf16[16,8,2048]{2,1,0:T(8,128)(2,1)} %fusion.1), calls=%async_computation.1 | async-start | bytes 1048576 | tf_op jit(solution)/shard_map/all_to_all | solution.py:145
  109.8 2.5 %grad_part.1 = bf16[256,384]{1,0:T(8,128)(2,1)} custom-call(bf16[8,256,128]{2,1,0:T(8,128)(2,1)} %all_to_all.35.cot_ref, bf16[8,128,384]{2,1,0:T(8,128)(2,1)} %all-to-all-done.5.act_ref), custom_call_target="tpu_custom_call" | custom-call | flops 201326592 | bytes 1048576 | tf_op jit(solution)/shard_map/grad_part/pallas_call | solution.py:121
  112.3 9.8 %all-to-all-done.1 = bf16[16,8,2048]{2,1,0:T(8,128)(2,1)S(1)} async-done(((bf16[16,8,2048]{2,1,0:T(8,128)(2,1)}), bf16[16,8,2048]{2,1,0:T(8,128)(2,1)S(1)}, u32[]{:S(2)}, u32[]{:S(2)}) %all-to-all-start.1) | async-done | bytes 524320 | tf_op jit(solution)/shard_map/all_to_all | solution.py:145
  122.1 18.6 %all-to-all-start.6 = ((bf16[8,32,384]{2,1,0:T(8,128)(2,1)}), bf16[8,32,384]{2,1,0:T(8,128)(2,1)S(1)}, u32[]{:S(2)}, u32[]{:S(2)}) async-start(bf16[8,32,384]{2,1,0:T(8,128)(2,1)} %bitcast.60), calls=%async_computation.6 | async-start | bytes 393216 | tf_op jit(solution)/shard_map/all_to_all | solution.py:145
  140.7 2.1 %combine_plain.1 = bf16[16,2048]{1,0:T(8,128)(2,1)} custom-call(s32[8,16]{1,0:T(8,128)} %bitcast.63, f32[8,16]{1,0:T(8,128)} %bitcast.65, bf16[128,2048]{1,0:T(8,128)(2,1)} %bitcast.15.rows_ref), custom_call_target="tpu_custom_call" | custom-call | flops 10000000 | bytes 524288 | tf_op jit(solution)/shard_map/combine_plain/pallas_call | solution.py:81
  142.8 0.0 copy-done.2
  142.8 2.2 %combine_weighted.1 = bf16[16,2048]{1,0:T(8,128)(2,1)} custom-call(s32[8,16]{1,0:T(8,128)} %bitcast.67, f32[8,16]{1,0:T(8,128)} %bitcast.69, bf16[128,2048]{1,0:T(8,128)(2,1)} %bitcast.58), custom_call_target="tpu_custom_call" | custom-call | flops 10000000 | bytes 524288 | tf_op jit(solution)/shard_map/combine_weighted/pallas_call | solution.py:81
  145.1 29.8 %all-to-all-done.6 = bf16[8,32,384]{2,1,0:T(8,128)(2,1)S(1)} async-done(((bf16[8,32,384]{2,1,0:T(8,128)(2,1)}), bf16[8,32,384]{2,1,0:T(8,128)(2,1)S(1)}, u32[]{:S(2)}, u32[]{:S(2)}) %all-to-all-start.6) | async-done | bytes 196640 | tf_op jit(solution)/shard_map/all_to_all | solution.py:145
  174.8 0.6 convert_reduce_fusion
  (6 shorter events, 0.0 us)
Async XLA Ops:
  0.6 12.2 %copy-start = (bf16[1,2048,384]{2,1,0:T(8,128)(2,1)S(1)}, bf16[1,2048,384]{2,1,0:T(8,128)(2,1)}, u32[]{:S(2)}) copy-start(bf16[1,2048,384]{2,1,0:T(8,128)(2,1)} %param.18) | copy-start | bytes 4718596
  0.6 10.6 %copy-start.1 = (bf16[1,2048,384]{2,1,0:T(8,128)(2,1)S(1)}, bf16[1,2048,384]{2,1,0:T(8,128)(2,1)}, u32[]{:S(2)}) copy-start(bf16[1,2048,384]{2,1,0:T(8,128)(2,1)} %param.17) | copy-start | bytes 4718596
  2.9 18.6 %all-to-all-start.2 = ((bf16[16,8,2048]{2,1,0:T(8,128)(2,1)}), bf16[16,8,2048]{2,1,0:T(8,128)(2,1)}, u32[]{:S(2)}, u32[]{:S(2)}) async-start(bf16[16,8,2048]{2,1,0:T(8,128)(2,1)} %bitcast.59), calls=%async_computation.2 | async-start | bytes 1048576 | tf_op jit(solution)/shard_map/all_to_all | solution.py:145
  11.2 1.6 copy-start.3
  21.5 16.6 %all-to-all-start = ((bf16[16,8,2048]{2,1,0:T(8,128)(2,1)}), bf16[16,8,2048]{2,1,0:T(8,128)(2,1)}, u32[]{:S(2)}, u32[]{:S(2)}) async-start(bf16[16,8,2048]{2,1,0:T(8,128)(2,1)} %bitcast.57), calls=%async_computation | async-start | bytes 1048576 | tf_op jit(solution)/shard_map/all_to_all | solution.py:145
  30.1 51.5 %copy-start.4 = (bf16[128,384]{1,0:T(8,128)(2,1)S(1)}, bf16[128,384]{1,0:T(8,128)(2,1)}, u32[]{:S(2)}) copy-start(bf16[128,384]{1,0:T(8,128)(2,1)} %get-tuple-element.3) | copy-start | bytes 294916
  38.1 16.6 %all-to-all-start.3 = ((bf16[16,8,2048]{2,1,0:T(8,128)(2,1)}), bf16[16,8,2048]{2,1,0:T(8,128)(2,1)}, u32[]{:S(2)}, u32[]{:S(2)}) async-start(bf16[16,8,2048]{2,1,0:T(8,128)(2,1)} %fusion.2), calls=%async_computation.3 | async-start | bytes 1048576 | tf_op jit(solution)/shard_map/all_to_all | solution.py:145
  82.5 22.9 %all-to-all-start.5 = ((bf16[8,128,384]{2,1,0:T(8,128)(2,1)}), bf16[8,128,384]{2,1,0:T(8,128)(2,1)}, u32[]{:S(2)}, u32[]{:S(2)}) async-start(bf16[8,128,384]{2,1,0:T(8,128)(2,1)} %broadcast_in_dim.4), calls=%async_computation.5 | async-start | bytes 1572864 | tf_op jit(solution)/shard_map/all_to_all | solution.py:145
  105.4 16.7 %all-to-all-start.1 = ((bf16[16,8,2048]{2,1,0:T(8,128)(2,1)}), bf16[16,8,2048]{2,1,0:T(8,128)(2,1)S(1)}, u32[]{:S(2)}, u32[]{:S(2)}) async-start(bf16[16,8,2048]{2,1,0:T(8,128)(2,1)} %fusion.1), calls=%async_computation.1 | async-start | bytes 1048576 | tf_op jit(solution)/shard_map/all_to_all | solution.py:145
  122.1 20.7 %copy-start.2 = (bf16[16,8,2048]{2,1,0:T(8,128)(2,1)}, bf16[16,8,2048]{2,1,0:T(8,128)(2,1)S(1)}, u32[]{:S(2)}) copy-start(bf16[16,8,2048]{2,1,0:T(8,128)(2,1)S(1)} %all-to-all-done.1) | copy-start | bytes 1572868
  122.1 52.7 %all-to-all-start.6 = ((bf16[8,32,384]{2,1,0:T(8,128)(2,1)}), bf16[8,32,384]{2,1,0:T(8,128)(2,1)S(1)}, u32[]{:S(2)}, u32[]{:S(2)}) async-start(bf16[8,32,384]{2,1,0:T(8,128)(2,1)} %bitcast.60), calls=%async_computation.6 | async-start | bytes 393216 | tf_op jit(solution)/shard_map/all_to_all | solution.py:145
